TPU v7x, 256 devices: a whole 4x4x8 slice. The times are simulated.
256 devices in a mesh: seq: 64 (over z, y, core), head: 4 (over x).
Axes of the slice: x: 4, y: 4, z: 8, core: 2. Of those that a mesh axis runs over, the one named last changes fastest.
Arguments:
- rotated_query_rows: bfloat16 [32768, 4096], P(('seq', 'head')), may hold values from -8 to 8
- rotated_key_rows: bfloat16 [32768, 2048], P(('seq', 'head')), may hold values from -8 to 8
- value_matrix: bfloat16 [32768, 2048], P(('seq', 'head')), may hold values from -6 to 6
- output_gradient: bfloat16 [32768, 4096], P(('seq', 'head')), may hold values from -6 to 6
- doc_lengths: int32 [64], replicated, may hold values from 1 to 2048, 32768 in all
Outputs:
- attended: bfloat16 [32768, 4096], P(('seq', 'head'))
- query_grad: bfloat16 [32768, 4096], P(('seq', 'head'))
- key_gradient: bfloat16 [32768, 2048], P(('seq', 'head'))
- value_gradient: bfloat16 [32768, 2048], P(('seq', 'head'))
Inputs may be any that keep to these rules, and one draw needn't show every extreme that they name: `doc_lengths`: the lengths of the 64 documents packed in order; they sum to 32768 and the longest has 2048 tokens.
All inputs are finite; a program needn't handle non-finite values.
Results may differ from a plain program's by a relative error of at most 0.02.
Values may be sent and summed in bfloat16 or wider, within the bound.
A program may use at most 128 MiB of HBM per device.

v0:
```python
import jax
import jax.numpy as jnp
from jax import lax
from jax.sharding import PartitionSpec as P

HEAD_WIDTH = 256
WINDOW_LENGTH = 1024
query_tile = 512


def passed_along(block, axis, distance):
    devices = range(lax.axis_size(axis))
    route = [(i - distance, i) for i in devices if i - distance in devices]
    return lax.ppermute(block, axis, route)


def doc_index(positions, doc_lengths):
    starts = jnp.cumsum(doc_lengths) - doc_lengths
    counted = jnp.sum((starts[None, :] <= positions[:, None]).astype(jnp.int32), axis=1)
    return counted - 1


def tile_pass(
    query_block, grad_block, key_block, value_block, query_docs, query_place, key_docs, key_place
):
    score_scale = HEAD_WIDTH ** (-0.5)
    scores = (
        jnp.einsum("qgd,kd->gqk", query_block, key_block, preferred_element_type=jnp.float32)
        * score_scale
    )
    offsets = query_place[:, None] - key_place[None, :]
    visible = (
        (query_docs[:, None] == key_docs[None, :]) & (offsets >= 0) & (offsets < WINDOW_LENGTH)
    )
    scores = jnp.where(visible[None], scores, -jnp.inf)
    row_max = jnp.max(scores, axis=2, keepdims=True)
    weights = jnp.exp(scores - row_max)
    probs_full = weights / jnp.sum(weights, axis=2, keepdims=True)
    probs_low = probs_full.astype(jnp.bfloat16)
    attended = jnp.einsum(
        "gqk,kd->qgd", probs_low, value_block, preferred_element_type=jnp.float32
    ).astype(jnp.bfloat16)
    row_delta = jnp.sum(grad_block.astype(jnp.float32) * attended.astype(jnp.float32), axis=2)
    value_part = jnp.einsum(
        "gqk,qgd->kd", probs_low, grad_block, preferred_element_type=jnp.float32
    )
    grad_probs = jnp.einsum(
        "qgd,kd->gqk", grad_block, value_block, preferred_element_type=jnp.float32
    )
    grad_low = (probs_full * (grad_probs - jnp.transpose(row_delta)[:, :, None])).astype(
        jnp.bfloat16
    )
    query_grad = (
        jnp.einsum("gqk,kd->qgd", grad_low, key_block, preferred_element_type=jnp.float32)
        * score_scale
    ).astype(jnp.bfloat16)
    key_part = (
        jnp.einsum("gqk,qgd->kd", grad_low, query_block, preferred_element_type=jnp.float32)
        * score_scale
    )
    return (attended, query_grad, key_part, value_part)


def head_sweep(query_head, grad_head, kv_head, key_docs, key_place, own_start):
    block_rows = query_head.shape[0]
    tile_rows = min(block_rows, query_tile)
    finish = own_start + tile_rows
    key_start = finish - tile_rows - WINDOW_LENGTH
    results = tile_pass(
        query_head,
        grad_head,
        kv_head[0, key_start:finish],
        kv_head[1, key_start:finish],
        key_docs[own_start:finish],
        key_place[own_start:finish],
        key_docs,
        key_place,
    )
    attended_tiles = results[0]
    grad_tiles = results[1]
    key_gradient_sums = results[2]
    value_gradient_sums = results[3]
    return (attended_tiles, grad_tiles, key_gradient_sums, value_gradient_sums)


def attend(exchanged, doc_lengths, group_width):
    query_parts, key_parts, value_parts, grad_parts = exchanged
    block_rows = query_parts.shape[0]
    head_items = query_parts.shape[2]
    kv_block = jnp.stack([key_parts[:, 0], value_parts[:, 0]], axis=0)
    rim_count = (WINDOW_LENGTH + block_rows - 2) // block_rows
    margin = max(0, WINDOW_LENGTH - rim_count * block_rows)
    rim_blocks = [passed_along(kv_block, "seq", distance) for distance in range(1, rim_count + 1)]
    pieces = (
        [jnp.zeros((2, margin, head_items, HEAD_WIDTH), jnp.bfloat16)]
        + rim_blocks[::-1]
        + [kv_block]
    )
    kv_window = jnp.concatenate(pieces, axis=1)
    own_start = margin + rim_count * block_rows
    key_length = own_start + block_rows
    key_place = (
        lax.axis_index("seq") * block_rows - own_start + jnp.arange(key_length, dtype=jnp.int32)
    )
    key_docs = doc_index(key_place, doc_lengths)
    outputs = []
    for head_item in range(head_items):
        query_head = query_parts[:, 0, head_item].reshape(block_rows, group_width, HEAD_WIDTH)
        grad_head = grad_parts[:, 0, head_item].reshape(block_rows, group_width, HEAD_WIDTH)
        kv_head = kv_window[:, :, head_item]
        swept_head = head_sweep(query_head, grad_head, kv_head, key_docs, key_place, own_start)
        outputs.append(swept_head)
    attended = jnp.stack([swept_head[0] for swept_head in outputs], axis=1).reshape(
        block_rows, 1, head_items, group_width * HEAD_WIDTH
    )
    query_grad = jnp.stack([swept_head[1] for swept_head in outputs], axis=1).reshape(
        block_rows, 1, head_items, group_width * HEAD_WIDTH
    )
    partial_grads = jnp.stack(
        [jnp.stack([swept_head[2], swept_head[3]], axis=0) for swept_head in outputs], axis=2
    )
    own_part = partial_grads[:, own_start:]
    gathered = own_part
    for distance in range(1, rim_count + 1):
        gathered = gathered + passed_along(
            partial_grads[
                :, own_start - distance * block_rows : own_start - (distance - 1) * block_rows
            ],
            "seq",
            -distance,
        )
    key_gradient = gathered[0].astype(jnp.bfloat16)[:, None]
    value_gradient = gathered[1].astype(jnp.bfloat16)[:, None]
    return (
        lax.all_to_all(attended, "head", split_axis=0, concat_axis=1, tiled=True),
        lax.all_to_all(query_grad, "head", split_axis=0, concat_axis=1, tiled=True),
        lax.all_to_all(key_gradient, "head", split_axis=0, concat_axis=1, tiled=True),
        lax.all_to_all(value_gradient, "head", split_axis=0, concat_axis=1, tiled=True),
    )


def shards(rotated_query_rows, rotated_key_rows, value_matrix, output_gradient, doc_lengths):
    token_total = rotated_query_rows.shape[0]
    groups_count = lax.axis_size("head")
    kv_count = rotated_key_rows.shape[1] // HEAD_WIDTH
    per_device = kv_count // groups_count
    group_width = rotated_query_rows.shape[1] // rotated_key_rows.shape[1]
    query_split = rotated_query_rows.reshape(
        token_total, groups_count, per_device, group_width * HEAD_WIDTH
    )
    key_split = rotated_key_rows.reshape(token_total, groups_count, per_device, HEAD_WIDTH)
    value_split = value_matrix.reshape(token_total, groups_count, per_device, HEAD_WIDTH)
    grad_split = output_gradient.reshape(
        token_total, groups_count, per_device, group_width * HEAD_WIDTH
    )
    attended, query_grad, key_gradient, value_gradient = attend(
        (
            lax.all_to_all(query_split, "head", split_axis=1, concat_axis=0, tiled=True),
            lax.all_to_all(key_split, "head", split_axis=1, concat_axis=0, tiled=True),
            lax.all_to_all(value_split, "head", split_axis=1, concat_axis=0, tiled=True),
            lax.all_to_all(grad_split, "head", split_axis=1, concat_axis=0, tiled=True),
        ),
        doc_lengths,
        group_width,
    )
    return (
        attended.reshape(token_total, rotated_query_rows.shape[1]),
        query_grad.reshape(token_total, rotated_query_rows.shape[1]),
        key_gradient.reshape(token_total, rotated_key_rows.shape[1]),
        value_gradient.reshape(token_total, rotated_key_rows.shape[1]),
    )


def solution(mesh):
    in_specs = (
        P(("seq", "head"), None),
        P(("seq", "head"), None),
        P(("seq", "head"), None),
        P(("seq", "head"), None),
        P(),
    )
    out_specs = (
        P(("seq", "head"), None),
        P(("seq", "head"), None),
        P(("seq", "head"), None),
        P(("seq", "head"), None),
    )
    return jax.shard_map(shards, mesh=mesh, in_specs=in_specs, out_specs=out_specs, check_vma=False)
```

profile of v0, /device:TPU:122, one launch (start us, length us, event | category | flops | bytes accessed | tf_op | source)
XLA Modules:
  0.0 237.3 jit_solution(12690508888914768315)
XLA Ops:
  3.1 4.8 %all-to-all-start = ((bf16[128,4,2,256]{3,0,2,1:T(8,128)(2,1)}), bf16[128,4,2,256]{3,0,2,1:T(8,128)(2,1)S(1)}, u32[]{:S(2)}, u32[]{:S(2)}) async-start(bf16[128,4,2,256]{3,0,2,1:T(8,128)(2,1)} %copy.160), calls=%async_computation | async-start | bytes 1048576 | tf_op jit(solution)/shard_map/all_to_all | solution.py:159
  9.2 6.7 %all-to-all-done = bf16[128,4,2,256]{3,0,2,1:T(8,128)(2,1)S(1)} async-done(((bf16[128,4,2,256]{3,0,2,1:T(8,128)(2,1)}), bf16[128,4,2,256]{3,0,2,1:T(8,128)(2,1)S(1)}, u32[]{:S(2)}, u32[]{:S(2)}) %all-to-all-start) | async-done | bytes 524320 | tf_op jit(solution)/shard_map/all_to_all | solution.py:159
  15.9 4.9 %all-to-all-start.1 = ((bf16[128,4,2,256]{3,0,2,1:T(8,128)(2,1)}), bf16[128,4,2,256]{3,0,2,1:T(8,128)(2,1)S(1)}, u32[]{:S(2)}, u32[]{:S(2)}) async-start(bf16[128,4,2,256]{3,0,2,1:T(8,128)(2,1)} %copy.163), calls=%async_computation.1 | async-start | bytes 1048576 | tf_op jit(solution)/shard_map/all_to_all | solution.py:160
  22.1 5.5 %all-to-all-done.1 = bf16[128,4,2,256]{3,0,2,1:T(8,128)(2,1)S(1)} async-done(((bf16[128,4,2,256]{3,0,2,1:T(8,128)(2,1)}), bf16[128,4,2,256]{3,0,2,1:T(8,128)(2,1)S(1)}, u32[]{:S(2)}, u32[]{:S(2)}) %all-to-all-start.1) | async-done | bytes 524320 | tf_op jit(solution)/shard_map/all_to_all | solution.py:160
  27.7 4.9 %all-to-all-start.2 = ((bf16[128,4,2,512]{0,3,2,1:T(8,128)(2,1)}), bf16[128,4,2,512]{0,3,2,1:T(8,128)(2,1)S(1)}, u32[]{:S(2)}, u32[]{:S(2)}) async-start(bf16[128,4,2,512]{0,3,2,1:T(8,128)(2,1)} %bitcast.13), calls=%async_computation.2 | async-start | bytes 2097152 | tf_op jit(solution)/shard_map/all_to_all | solution.py:158
  38.1 5.7 %all-to-all-done.2 = bf16[128,4,2,512]{0,3,2,1:T(8,128)(2,1)S(1)} async-done(((bf16[128,4,2,512]{0,3,2,1:T(8,128)(2,1)}), bf16[128,4,2,512]{0,3,2,1:T(8,128)(2,1)S(1)}, u32[]{:S(2)}, u32[]{:S(2)}) %all-to-all-start.2) | async-done | bytes 1048608 | tf_op jit(solution)/shard_map/all_to_all | solution.py:158
  43.8 5.1 %all-to-all-start.4 = ((bf16[128,4,2,512]{3,2,0,1:T(2,128)(2,1)}), bf16[128,4,2,512]{3,2,0,1:T(2,128)(2,1)S(1)}, u32[]{:S(2)}, u32[]{:S(2)}) async-start(bf16[128,4,2,512]{3,2,0,1:T(2,128)(2,1)} %copy.180), calls=%async_computation.4 | async-start | bytes 2097152 | tf_op jit(solution)/shard_map/all_to_all | solution.py:161
  51.9 4.7 %collective-permute-start = (bf16[2,512,2,256]{3,1,2,0:T(8,128)(2,1)}, bf16[2,512,2,256]{3,1,2,0:T(8,128)(2,1)}, u32[]{:S(2)}, u32[]{:S(2)}) collective-permute-start(bf16[2,512,2,256]{3,1,2,0:T(8,128)(2,1)} %pad_maximum_fusion.1), channel_id=1, source_target_pairs={{0,8},{4,12},{8,16},{12,20},{16,24},{20,28},{24,32},{28,36},{32,40... | collective-permute-start | bytes 3145736 | tf_op jit(solution)/shard_map/ppermute | solution.py:14
  69.4 5.7 %collective-permute-done.1 = bf16[2,512,2,256]{3,1,2,0:T(8,128)(2,1)} collective-permute-done((bf16[2,512,2,256]{3,1,2,0:T(8,128)(2,1)}, bf16[2,512,2,256]{3,1,2,0:T(8,128)(2,1)}, u32[]{:S(2)}, u32[]{:S(2)}) %collective-permute-start.1) | collective-permute-done | bytes 1048608 | tf_op jit(solution)/shard_map/ppermute | solution.py:14
  75.1 5.4 %collective-permute-done = bf16[2,512,2,256]{3,1,2,0:T(8,128)(2,1)} collective-permute-done((bf16[2,512,2,256]{3,1,2,0:T(8,128)(2,1)}, bf16[2,512,2,256]{3,1,2,0:T(8,128)(2,1)}, u32[]{:S(2)}, u32[]{:S(2)}) %collective-permute-start) | collective-permute-done | bytes 1048608 | tf_op jit(solution)/shard_map/ppermute | solution.py:14
  82.7 7.3 %fusion.42 = (f32[2,512]{1,0:T(2,128)S(1)}, f32[2,512,1536]{1,2,0:T(8,128)}) fusion(pred[512,1536]{0,1:T(8,128)(4,1)} %fusion.13, bf16[512,2,256]{0,2,1:T(8,128)(2,1)} %bitcast.208, bf16[2,1536,2,256]{3,1,2,0:T(8,128)(2,1)S(1)} %maximum_maximum_fusion), kind=kOutput, calls=%fused_computation.80 | convolution fusion | flops 811599360 | bytes 8392704 | tf_op jit(solution)/shard_map/sub | solution.py:37
  97.7 6.3 %fusion.41 = (f32[2,512]{1,0:T(2,128)S(1)}, f32[2,512,1536]{1,2,0:T(8,128)}) fusion(pred[512,1536]{0,1:T(8,128)(4,1)} %fusion.13, bf16[512,2,256]{0,2,1:T(8,128)(2,1)} %bitcast.206, bf16[2,1536,2,256]{3,1,2,0:T(8,128)(2,1)S(1)} %maximum_maximum_fusion), kind=kOutput, calls=%fused_computation.79 | convolution fusion | flops 811599360 | bytes 8392704 | tf_op jit(solution)/shard_map/sub | solution.py:37
  104.0 3.8 %fusion.21 = bf16[2,512,1536]{1,2,0:T(8,128)(2,1)S(1)} fusion(f32[2,512,1536]{1,2,0:T(8,128)} %get-tuple-element.13, f32[2,512]{1,0:T(2,128)S(1)} %get-tuple-element.12), kind=kLoop, calls=%fused_computation.42 | loop fusion | flops 3145728 | bytes 9441280 | tf_op jit(solution)/shard_map/convert_element_type | solution.py:39
  121.6 10.4 %collective-permute-start.2 = (f32[2,512,2,256]{3,1,0,2:T(8,128)}, f32[2,512,2,256]{3,1,0,2:T(8,128)}, u32[]{:S(2)}, u32[]{:S(2)}) collective-permute-start(f32[2,512,2,256]{3,1,0,2:T(8,128)} %get-tuple-element.4), channel_id=1, source_target_pairs={{4,0},{8,4},{12,8},{16,12},{20,16},{24,20},{28,24},{32,28},{36,32}... | collective-permute-start | bytes 6291464 | tf_op jit(solution)/shard_map/ppermute | solution.py:14
  141.5 4.2 %pad_maximum_fusion.2 = bf16[512,1,2,512]{3,2,1,0:T(2,128)(2,1)} fusion(bf16[512,1,1,512]{3,2,1,0:T(2,128)(2,1)} %copy.177, bf16[512,1,1,512]{3,2,1,0:T(2,128)(2,1)} %copy.176), kind=kLoop, calls=%fused_computation.56 | loop fusion | flops 2097152 | bytes 2097152 | tf_op jit(solution)/shard_map/stack | solution.py:113
  145.7 4.8 %all-to-all-start.3 = ((bf16[512,1,2,512]{3,2,1,0:T(2,128)(2,1)}), bf16[512,1,2,512]{3,2,1,0:T(2,128)(2,1)}, u32[]{:S(2)}, u32[]{:S(2)}) async-start(bf16[512,1,2,512]{3,2,1,0:T(2,128)(2,1)} %pad_maximum_fusion.2), calls=%async_computation.3 | async-start | bytes 2097152 | tf_op jit(solution)/shard_map/all_to_all | solution.py:135
  150.5 3.9 %fusion.27 = bf16[256,2,512]{2,0,1:T(8,128)(2,1)} fusion(bf16[2,512,1536]{1,2,0:T(8,128)(2,1)} %copy-done.4, bf16[2,1536,2,256]{3,1,2,0:T(8,128)(2,1)} %copy-done.1), kind=kOutput, calls=%fused_computation.51 | convolution fusion | flops 805830656 | bytes 4456448 | tf_op jit(solution)/shard_map/gqk,kd->qgd/dot_general | solution.py:54
  158.0 3.9 %fusion.28 = bf16[256,2,512]{2,0,1:T(8,128)(2,1)} fusion(bf16[2,512,1536]{1,2,0:T(8,128)(2,1)} %copy-done.5, bf16[2,1536,2,256]{3,1,2,0:T(8,128)(2,1)} %copy-done.1), kind=kOutput, calls=%fused_computation.52 | convolution fusion | flops 805830656 | bytes 4456448 | tf_op jit(solution)/shard_map/gqk,kd->qgd/dot_general | solution.py:54
  165.5 4.2 %pad_maximum_fusion.3 = bf16[512,1,2,512]{3,2,1,0:T(2,128)(2,1)} fusion(bf16[512,1,1,512]{3,2,1,0:T(2,128)(2,1)} %copy.190, bf16[512,1,1,512]{3,2,1,0:T(2,128)(2,1)} %copy.189), kind=kLoop, calls=%fused_computation.57 | loop fusion | flops 2097152 | bytes 2097152 | tf_op jit(solution)/shard_map/stack | solution.py:116
  169.7 4.8 %all-to-all-start.5 = ((bf16[512,1,2,512]{3,2,1,0:T(2,128)(2,1)}), bf16[512,1,2,512]{3,2,1,0:T(2,128)(2,1)}, u32[]{:S(2)}, u32[]{:S(2)}) async-start(bf16[512,1,2,512]{3,2,1,0:T(2,128)(2,1)} %pad_maximum_fusion.3), calls=%async_computation.5 | async-start | bytes 2097152 | tf_op jit(solution)/shard_map/all_to_all | solution.py:136
  176.7 29.7 %collective-permute-done.3 = f32[2,512,2,256]{3,1,0,2:T(8,128)} collective-permute-done((f32[2,512,2,256]{3,1,0,2:T(8,128)}, f32[2,512,2,256]{3,1,0,2:T(8,128)}, u32[]{:S(2)}, u32[]{:S(2)}) %collective-permute-start.3) | collective-permute-done | bytes 2097184 | tf_op jit(solution)/shard_map/ppermute | solution.py:14
  210.7 4.8 %all-to-all-start.7 = ((bf16[512,1,2,256]{3,2,1,0:T(2,128)(2,1)}), bf16[512,1,2,256]{3,2,1,0:T(2,128)(2,1)S(1)}, u32[]{:S(2)}, u32[]{:S(2)}) async-start(bf16[512,1,2,256]{3,2,1,0:T(2,128)(2,1)} %copy.198), calls=%async_computation.7 | async-start | bytes 1048576 | tf_op jit(solution)/shard_map/all_to_all | solution.py:138
  216.8 5.3 %all-to-all-done.7 = bf16[512,1,2,256]{3,2,1,0:T(2,128)(2,1)S(1)} async-done(((bf16[512,1,2,256]{3,2,1,0:T(2,128)(2,1)}), bf16[512,1,2,256]{3,2,1,0:T(2,128)(2,1)S(1)}, u32[]{:S(2)}, u32[]{:S(2)}) %all-to-all-start.7) | async-done | bytes 524320 | tf_op jit(solution)/shard_map/all_to_all | solution.py:138
  222.1 4.9 %all-to-all-start.6 = ((bf16[512,1,2,256]{3,2,1,0:T(2,128)(2,1)}), bf16[512,1,2,256]{3,2,1,0:T(2,128)(2,1)S(1)}, u32[]{:S(2)}, u32[]{:S(2)}) async-start(bf16[512,1,2,256]{3,2,1,0:T(2,128)(2,1)} %copy.196), calls=%async_computation.6 | async-start | bytes 1048576 | tf_op jit(solution)/shard_map/all_to_all | solution.py:137
  (114 shorter events, 84.2 us)
Async XLA Ops:
  0.6 7.3 %copy-start.12 = (bf16[128,2048]{1,0:T(8,128)(2,1)S(1)}, bf16[128,2048]{1,0:T(8,128)(2,1)}, u32[]{:S(2)}) copy-start(bf16[128,2048]{1,0:T(8,128)(2,1)} %param.7) | copy-start | bytes 1572868
  0.6 20.2 %copy-start.11 = (bf16[128,4096]{1,0:T(8,128)(2,1)S(1)}, bf16[128,4096]{1,0:T(8,128)(2,1)}, u32[]{:S(2)}) copy-start(bf16[128,4096]{1,0:T(8,128)(2,1)} %param.5) | copy-start | bytes 3145732
  3.1 12.8 %all-to-all-start = ((bf16[128,4,2,256]{3,0,2,1:T(8,128)(2,1)}), bf16[128,4,2,256]{3,0,2,1:T(8,128)(2,1)S(1)}, u32[]{:S(2)}, u32[]{:S(2)}) async-start(bf16[128,4,2,256]{3,0,2,1:T(8,128)(2,1)} %copy.160), calls=%async_computation | async-start | bytes 1048576 | tf_op jit(solution)/shard_map/all_to_all | solution.py:159
  8.2 24.4 %copy-start.19 = (s32[64]{0:T(128)S(1)}, s32[64]{0:T(128)}, u32[]{:S(2)}) copy-start(s32[64]{0:T(128)} %param.9) | copy-start | bytes 772
  15.9 11.7 %all-to-all-start.1 = ((bf16[128,4,2,256]{3,0,2,1:T(8,128)(2,1)}), bf16[128,4,2,256]{3,0,2,1:T(8,128)(2,1)S(1)}, u32[]{:S(2)}, u32[]{:S(2)}) async-start(bf16[128,4,2,256]{3,0,2,1:T(8,128)(2,1)} %copy.163), calls=%async_computation.1 | async-start | bytes 1048576 | tf_op jit(solution)/shard_map/all_to_all | solution.py:160
  27.7 16.2 %all-to-all-start.2 = ((bf16[128,4,2,512]{0,3,2,1:T(8,128)(2,1)}), bf16[128,4,2,512]{0,3,2,1:T(8,128)(2,1)S(1)}, u32[]{:S(2)}, u32[]{:S(2)}) async-start(bf16[128,4,2,512]{0,3,2,1:T(8,128)(2,1)} %bitcast.13), calls=%async_computation.2 | async-start | bytes 2097152 | tf_op jit(solution)/shard_map/all_to_all | solution.py:158
  32.6 5.4 %copy-start.15 = (s32[1536]{0:T(1024)}, s32[1536]{0:T(1024)S(1)}, u32[]{:S(2)}) copy-start(s32[1536]{0:T(1024)S(1)} %iota_add_fusion) | copy-start | bytes 18436
  36.8 23.3 %copy-start.2 = (bf16[4,128,1,2,256]{4,1,0,3,2:T(8,128)(2,1)}, bf16[4,128,1,2,256]{4,1,0,3,2:T(8,128)(2,1)S(1)}, u32[]{:S(2)}) copy-start(bf16[4,128,1,2,256]{4,1,0,3,2:T(8,128)(2,1)S(1)} %copy.161) | copy-start | bytes 1572868
  38.1 22.0 %copy-start.3 = (bf16[4,128,1,2,256]{4,1,0,3,2:T(8,128)(2,1)}, bf16[4,128,1,2,256]{4,1,0,3,2:T(8,128)(2,1)S(1)}, u32[]{:S(2)}) copy-start(bf16[4,128,1,2,256]{4,1,0,3,2:T(8,128)(2,1)S(1)} %copy.164) | copy-start | bytes 1572868
  43.8 12.8 %copy-start.16 = (s32[1536]{0:T(1024)S(1)}, s32[1536]{0:T(1024)}, u32[]{:S(2)}) copy-start(s32[1536]{0:T(1024)} %copy-done.15) | copy-start | bytes 18436
  43.8 12.8 %slice-start.4 = ((s32[1536]{0:T(1024)}), s32[512]{0:T(512)S(1)}, s32[]{:S(2)}) async-start(s32[1536]{0:T(1024)} %copy-done.15), calls=%async_computation.12 | async-start | bytes 4096 | tf_op jit(solution)/shard_map/slice | solution.py:75
  43.8 12.8 %copy-start.18 = (s32[1536]{0:T(1024)S(1)}, s32[1536]{0:T(1024)}, u32[]{:S(2)}) copy-start(s32[1536]{0:T(1024)} %copy-done.17) | copy-start | bytes 18436
  43.8 12.8 %slice-start.5 = ((s32[1536]{0:T(1024)}), s32[512]{0:T(512)S(1)}, s32[]{:S(2)}) async-start(s32[1536]{0:T(1024)} %copy-done.17), calls=%async_computation.13 | async-start | bytes 4096 | tf_op jit(solution)/shard_map/slice | solution.py:74
  43.8 19.5 %all-to-all-start.4 = ((bf16[128,4,2,512]{3,2,0,1:T(2,128)(2,1)}), bf16[128,4,2,512]{3,2,0,1:T(2,128)(2,1)S(1)}, u32[]{:S(2)}, u32[]{:S(2)}) async-start(bf16[128,4,2,512]{3,2,0,1:T(2,128)(2,1)} %copy.180), calls=%async_computation.4 | async-start | bytes 2097152 | tf_op jit(solution)/shard_map/all_to_all | solution.py:161
  50.0 25.1 %collective-permute-start.1 = (bf16[2,512,2,256]{3,1,2,0:T(8,128)(2,1)}, bf16[2,512,2,256]{3,1,2,0:T(8,128)(2,1)}, u32[]{:S(2)}, u32[]{:S(2)}) collective-permute-start(bf16[2,512,2,256]{3,1,2,0:T(8,128)(2,1)} %pad_maximum_fusion.1), channel_id=1, source_target_pairs={{0,4},{4,8},{8,12},{12,16},{16,20},{20,24},{24,28},{28,32},{32,36}... | collective-permute-start | bytes 3145736 | tf_op jit(solution)/shard_map/ppermute | solution.py:14
  51.9 28.6 %collective-permute-start = (bf16[2,512,2,256]{3,1,2,0:T(8,128)(2,1)}, bf16[2,512,2,256]{3,1,2,0:T(8,128)(2,1)}, u32[]{:S(2)}, u32[]{:S(2)}) collective-permute-start(bf16[2,512,2,256]{3,1,2,0:T(8,128)(2,1)} %pad_maximum_fusion.1), channel_id=1, source_target_pairs={{0,8},{4,12},{8,16},{12,20},{16,24},{20,28},{24,32},{28,36},{32,40... | collective-permute-start | bytes 3145736 | tf_op jit(solution)/shard_map/ppermute | solution.py:14
  82.7 31.1 %copy-start.1 = (bf16[2,1536,2,256]{3,1,2,0:T(8,128)(2,1)}, bf16[2,1536,2,256]{3,1,2,0:T(8,128)(2,1)S(1)}, u32[]{:S(2)}) copy-start(bf16[2,1536,2,256]{3,1,2,0:T(8,128)(2,1)S(1)} %maximum_maximum_fusion) | copy-start | bytes 9437188
  104.0 6.7 %slice-start = ((s8[6291456]{0:T(1024)(128)(4,1)}), s8[4194304]{0:T(1024)(128)(4,1)S(1)}, s32[]{:S(2)}) async-start(s8[6291456]{0:T(1024)(128)(4,1)} %bitcast.179), calls=%async_computation.8 | async-start | bytes 8388608
  121.6 55.2 %collective-permute-start.2 = (f32[2,512,2,256]{3,1,0,2:T(8,128)}, f32[2,512,2,256]{3,1,0,2:T(8,128)}, u32[]{:S(2)}, u32[]{:S(2)}) collective-permute-start(f32[2,512,2,256]{3,1,0,2:T(8,128)} %get-tuple-element.4), channel_id=1, source_target_pairs={{4,0},{8,4},{12,8},{16,12},{20,16},{24,20},{28,24},{32,28},{36,32}... | collective-permute-start | bytes 6291464 | tf_op jit(solution)/shard_map/ppermute | solution.py:14
  132.0 74.4 %collective-permute-start.3 = (f32[2,512,2,256]{3,1,0,2:T(8,128)}, f32[2,512,2,256]{3,1,0,2:T(8,128)}, u32[]{:S(2)}, u32[]{:S(2)}) collective-permute-start(f32[2,512,2,256]{3,1,0,2:T(8,128)} %get-tuple-element.5), channel_id=1, source_target_pairs={{8,0},{12,4},{16,8},{20,12},{24,16},{28,20},{32,24},{36,28},{40,32... | collective-permute-start | bytes 6291464 | tf_op jit(solution)/shard_map/ppermute | solution.py:14
  145.7 24.0 %all-to-all-start.3 = ((bf16[512,1,2,512]{3,2,1,0:T(2,128)(2,1)}), bf16[512,1,2,512]{3,2,1,0:T(2,128)(2,1)}, u32[]{:S(2)}, u32[]{:S(2)}) async-start(bf16[512,1,2,512]{3,2,1,0:T(2,128)(2,1)} %pad_maximum_fusion.2), calls=%async_computation.3 | async-start | bytes 2097152 | tf_op jit(solution)/shard_map/all_to_all | solution.py:135
  169.7 41.0 %all-to-all-start.5 = ((bf16[512,1,2,512]{3,2,1,0:T(2,128)(2,1)}), bf16[512,1,2,512]{3,2,1,0:T(2,128)(2,1)}, u32[]{:S(2)}, u32[]{:S(2)}) async-start(bf16[512,1,2,512]{3,2,1,0:T(2,128)(2,1)} %pad_maximum_fusion.3), calls=%async_computation.5 | async-start | bytes 2097152 | tf_op jit(solution)/shard_map/all_to_all | solution.py:136
  210.7 11.4 %all-to-all-start.7 = ((bf16[512,1,2,256]{3,2,1,0:T(2,128)(2,1)}), bf16[512,1,2,256]{3,2,1,0:T(2,128)(2,1)S(1)}, u32[]{:S(2)}, u32[]{:S(2)}) async-start(bf16[512,1,2,256]{3,2,1,0:T(2,128)(2,1)} %copy.198), calls=%async_computation.7 | async-start | bytes 1048576 | tf_op jit(solution)/shard_map/all_to_all | solution.py:138
  222.1 13.6 %all-to-all-start.6 = ((bf16[512,1,2,256]{3,2,1,0:T(2,128)(2,1)}), bf16[512,1,2,256]{3,2,1,0:T(2,128)(2,1)S(1)}, u32[]{:S(2)}, u32[]{:S(2)}) async-start(bf16[512,1,2,256]{3,2,1,0:T(2,128)(2,1)} %copy.196), calls=%async_computation.6 | async-start | bytes 1048576 | tf_op jit(solution)/shard_map/all_to_all | solution.py:137
  (14 other events, 41.1 us)
where the time goes:
time: 239 us; the launch traced here: 237 us
  waiting for transfers between devices  66.4 us (28%)
  starting transfers between devices  58.5 us (24%)
  local copies, waits for them, and re-layouts  51.2 us (21%)
  matrix products  32.6 us (14%)
  other arithmetic  27.6 us (12%)
    ppermute x4, waiting for transfers between devices, passed_along(): return lax.ppermute(block, axis, route)  43.1 us
    ppermute x4, starting transfers between devices, passed_along(): return lax.ppermute(block, axis, route)  19.4 us
    sub x2, matrix products, tile_pass(): weights = jnp.exp(scores - row_max)  13.6 us
    unnamed x54, local copies, waits for them, and re-layouts  12.5 us
    dot_general x2, matrix products, tile_pass(): jnp.einsum('gqk,kd->qgd', grad_low, key_block, preferred_element_type=jnp...  7.86 us
    convert_element_type x2, other arithmetic, tile_pass(): probs_low = probs_full.astype(jnp.bfloat16)  7.57 us
    another operation x2, local copies, waits for them, and re-layouts, attend(): jnp.stack([swept_head[0] for swept_head in outputs], axis=1)  7.13 us
    another operation x2, local copies, waits for them, and re-layouts, attend(): jnp.stack([swept_head[1] for swept_head in outputs], axis=1)  7.12 us
  transfers between devices with their start and end apart: 12, of which 8 were waited for; matrix products, arithmetic and copies ran while one was open for 28% of the time, Pallas kernels for 0%

commit v1 on v0

--- a/solution.py
+++ b/solution.py
@@ -6,6 +6,22 @@
 HEAD_WIDTH = 256
 WINDOW_LENGTH = 1024
 query_tile = 512
+
+
+def pairwise_exchange(array, axis, split, join):
+    ways, here = (lax.axis_size(axis), lax.axis_index(axis))
+    width = array.shape[split] // ways
+    shape = list(array.shape)
+    shape[split] = width
+    height = shape[join]
+    shape[join] = height * ways
+    full = jnp.zeros(shape, array.dtype)
+    for mask in range(ways):
+        part = lax.dynamic_slice_in_dim(array, (here ^ mask) * width, width, axis=split)
+        if mask:
+            part = lax.ppermute(part, axis, [(d, d ^ mask) for d in range(ways)])
+        full = lax.dynamic_update_slice_in_dim(full, part, (here ^ mask) * height, axis=join)
+    return full
 
 
 def passed_along(block, axis, distance):
@@ -158,7 +174,7 @@
             lax.all_to_all(query_split, "head", split_axis=1, concat_axis=0, tiled=True),
             lax.all_to_all(key_split, "head", split_axis=1, concat_axis=0, tiled=True),
             lax.all_to_all(value_split, "head", split_axis=1, concat_axis=0, tiled=True),
-            lax.all_to_all(grad_split, "head", split_axis=1, concat_axis=0, tiled=True),
+            pairwise_exchange(grad_split, "head", 1, 0),
         ),
         doc_lengths,
         group_width,

time: 239 us -> 229 us (0.958)
  local copies, waits for them, and re-layouts: 51.2 us -> 44.8 us
  waiting for transfers between devices: 66.4 us -> 62.7 us
    all_to_all x1, waiting for transfers between devices: 5.74 us -> 0.01 us  [shards(): lax.all_to_all(query_split, 'head', split_axis=1, concat_axis=0, tiled=True)]
    all_to_all x1 -> x0, starting transfers between devices: 5.09 us -> none  [shards(): lax.all_to_all(grad_split, 'head', split_axis=1, concat_axis=0, tiled=True)]
    ppermute x4, waiting for transfers between devices: 43.1 us -> 48 us  [passed_along(): return lax.ppermute(block, axis, route)]
    unnamed x54 -> x41, local copies, waits for them, and re-layouts: 12.5 us -> 8.02 us
    ppermute x0 -> x3, starting transfers between devices: none -> 4.09 us  [pairwise_exchange(): part = lax.ppermute(part, axis, [(d, d ^ mask) for d in range(ways)])]
  transfers between devices with their start and end apart: 12 -> 14, of which waited for: 8 -> 7; matrix products, arithmetic and copies ran while one was open for 28% -> 26% of each run, Pallas kernels for 0% -> 0%
where the time goes in v1:
time: 229 us; the launch traced here: 228 us
  waiting for transfers between devices  62.7 us (27%)
  starting transfers between devices  59 us (26%)
  local copies, waits for them, and re-layouts  44.8 us (20%)
  matrix products  32.5 us (14%)
  other arithmetic  27.6 us (12%)
    ppermute x4, waiting for transfers between devices, passed_along(): return lax.ppermute(block, axis, route)  48 us
    ppermute x4, starting transfers between devices, passed_along(): return lax.ppermute(block, axis, route)  19.4 us
    sub x2, matrix products, tile_pass(): weights = jnp.exp(scores - row_max)  13.6 us
    unnamed x41, local copies, waits for them, and re-layouts  8.02 us
    dot_general x2, matrix products, tile_pass(): jnp.einsum('gqk,kd->qgd', grad_low, key_block, preferred_element_type=jnp...  7.86 us
    convert_element_type x2, other arithmetic, tile_pass(): probs_low = probs_full.astype(jnp.bfloat16)  7.57 us
    another operation x2, local copies, waits for them, and re-layouts, attend(): jnp.stack([swept_head[0] for swept_head in outputs], axis=1)  7.13 us
    another operation x2, local copies, waits for them, and re-layouts, attend(): jnp.stack([swept_head[1] for swept_head in outputs], axis=1)  7.12 us
  transfers between devices with their start and end apart: 14, of which 7 were waited for; matrix products, arithmetic and copies ran while one was open for 26% of the time, Pallas kernels for 0%

profile of v1, /device:TPU:122, one launch (start us, length us, event | category | flops | bytes accessed | tf_op | source)
XLA Modules:
  0.0 227.7 jit_solution(5332028876851084163)
XLA Ops:
  3.1 5.0 %all-to-all-start = ((bf16[128,4,2,256]{3,0,2,1:T(8,128)(2,1)}), bf16[128,4,2,256]{3,0,2,1:T(8,128)(2,1)S(1)}, u32[]{:S(2)}, u32[]{:S(2)}) async-start(bf16[128,4,2,256]{3,0,2,1:T(8,128)(2,1)} %copy.171), calls=%async_computation | async-start | bytes 1048576 | tf_op jit(solution)/shard_map/all_to_all | solution.py:175
  15.2 5.5 %all-to-all-done = bf16[128,4,2,256]{3,0,2,1:T(8,128)(2,1)S(1)} async-done(((bf16[128,4,2,256]{3,0,2,1:T(8,128)(2,1)}), bf16[128,4,2,256]{3,0,2,1:T(8,128)(2,1)S(1)}, u32[]{:S(2)}, u32[]{:S(2)}) %all-to-all-start) | async-done | bytes 524320 | tf_op jit(solution)/shard_map/all_to_all | solution.py:175
  20.7 6.3 %all-to-all-start.1 = ((bf16[128,4,2,256]{3,0,2,1:T(8,128)(2,1)}), bf16[128,4,2,256]{3,0,2,1:T(8,128)(2,1)S(1)}, u32[]{:S(2)}, u32[]{:S(2)}) async-start(bf16[128,4,2,256]{3,0,2,1:T(8,128)(2,1)} %copy.174), calls=%async_computation.1 | async-start | bytes 1048576 | tf_op jit(solution)/shard_map/all_to_all | solution.py:176
  29.8 3.8 %all-to-all-done.1 = bf16[128,4,2,256]{3,0,2,1:T(8,128)(2,1)S(1)} async-done(((bf16[128,4,2,256]{3,0,2,1:T(8,128)(2,1)}), bf16[128,4,2,256]{3,0,2,1:T(8,128)(2,1)S(1)}, u32[]{:S(2)}, u32[]{:S(2)}) %all-to-all-start.1) | async-done | bytes 524320 | tf_op jit(solution)/shard_map/all_to_all | solution.py:176
  33.6 4.9 %all-to-all-start.2 = ((bf16[128,4,2,512]{0,3,2,1:T(8,128)(2,1)}), bf16[128,4,2,512]{0,3,2,1:T(8,128)(2,1)S(1)}, u32[]{:S(2)}, u32[]{:S(2)}) async-start(bf16[128,4,2,512]{0,3,2,1:T(8,128)(2,1)} %bitcast.13), calls=%async_computation.2 | async-start | bytes 2097152 | tf_op jit(solution)/shard_map/all_to_all | solution.py:174
  42.4 4.7 %collective-permute-start = (bf16[2,512,2,256]{3,1,2,0:T(8,128)(2,1)}, bf16[2,512,2,256]{3,1,2,0:T(8,128)(2,1)}, u32[]{:S(2)}, u32[]{:S(2)}) collective-permute-start(bf16[2,512,2,256]{3,1,2,0:T(8,128)(2,1)} %pad_maximum_fusion.1), channel_id=1, source_target_pairs={{0,8},{4,12},{8,16},{12,20},{16,24},{20,28},{24,32},{28,36},{32,40... | collective-permute-start | bytes 3145736 | tf_op jit(solution)/shard_map/ppermute | solution.py:30
  55.0 10.6 %collective-permute-done.1 = bf16[2,512,2,256]{3,1,2,0:T(8,128)(2,1)} collective-permute-done((bf16[2,512,2,256]{3,1,2,0:T(8,128)(2,1)}, bf16[2,512,2,256]{3,1,2,0:T(8,128)(2,1)}, u32[]{:S(2)}, u32[]{:S(2)}) %collective-permute-start.1) | collective-permute-done | bytes 1048608 | tf_op jit(solution)/shard_map/ppermute | solution.py:30
  65.6 5.4 %collective-permute-done = bf16[2,512,2,256]{3,1,2,0:T(8,128)(2,1)} collective-permute-done((bf16[2,512,2,256]{3,1,2,0:T(8,128)(2,1)}, bf16[2,512,2,256]{3,1,2,0:T(8,128)(2,1)}, u32[]{:S(2)}, u32[]{:S(2)}) %collective-permute-start) | collective-permute-done | bytes 1048608 | tf_op jit(solution)/shard_map/ppermute | solution.py:30
  73.2 7.2 %fusion.42 = (f32[2,512]{1,0:T(2,128)S(1)}, f32[2,512,1536]{1,2,0:T(8,128)}) fusion(pred[512,1536]{0,1:T(8,128)(4,1)} %fusion.13, bf16[512,2,256]{0,2,1:T(8,128)(2,1)} %bitcast.202, bf16[2,1536,2,256]{3,1,2,0:T(8,128)(2,1)S(1)} %maximum_maximum_fusion), kind=kOutput, calls=%fused_computation.87 | convolution fusion | flops 811599360 | bytes 8392704 | tf_op jit(solution)/shard_map/sub | solution.py:53
  80.4 3.7 %fusion.20 = bf16[2,512,1536]{1,2,0:T(8,128)(2,1)S(1)} fusion(f32[2,512,1536]{1,2,0:T(8,128)} %get-tuple-element.19, f32[2,512]{1,0:T(2,128)S(1)} %get-tuple-element.18), kind=kLoop, calls=%fused_computation.41 | loop fusion | flops 3145728 | bytes 9441280 | tf_op jit(solution)/shard_map/convert_element_type | solution.py:55
  88.1 6.3 %fusion.41 = (f32[2,512]{1,0:T(2,128)S(1)}, f32[2,512,1536]{1,2,0:T(8,128)}) fusion(pred[512,1536]{0,1:T(8,128)(4,1)} %fusion.13, bf16[512,2,256]{0,2,1:T(8,128)(2,1)} %bitcast.200, bf16[2,1536,2,256]{3,1,2,0:T(8,128)(2,1)S(1)} %maximum_maximum_fusion), kind=kOutput, calls=%fused_computation.86 | convolution fusion | flops 811599360 | bytes 8392704 | tf_op jit(solution)/shard_map/sub | solution.py:53
  94.4 3.8 %fusion.21 = bf16[2,512,1536]{1,2,0:T(8,128)(2,1)S(1)} fusion(f32[2,512,1536]{1,2,0:T(8,128)} %get-tuple-element.17, f32[2,512]{1,0:T(2,128)S(1)} %get-tuple-element.16), kind=kLoop, calls=%fused_computation.42 | loop fusion | flops 3145728 | bytes 9441280 | tf_op jit(solution)/shard_map/convert_element_type | solution.py:55
  112.1 10.4 %collective-permute-start.5 = (f32[2,512,2,256]{3,1,0,2:T(8,128)}, f32[2,512,2,256]{3,1,0,2:T(8,128)}, u32[]{:S(2)}, u32[]{:S(2)}) collective-permute-start(f32[2,512,2,256]{3,1,0,2:T(8,128)} %get-tuple-element.4), channel_id=1, source_target_pairs={{4,0},{8,4},{12,8},{16,12},{20,16},{24,20},{28,24},{32,28},{36,32}... | collective-permute-start | bytes 6291464 | tf_op jit(solution)/shard_map/ppermute | solution.py:30
  124.9 3.6 %copy.187 = bf16[512,1,1,512]{3,2,1,0:T(2,128)(2,1)} copy(bf16[512,1,1,512]{0,3,2,1:T(8,128)(2,1)} %bitcast.192) | data formatting | bytes 1048576 | tf_op jit(solution)/shard_map/stack | solution.py:129
  132.0 4.2 %pad_maximum_fusion.2 = bf16[512,1,2,512]{3,2,1,0:T(2,128)(2,1)} fusion(bf16[512,1,1,512]{3,2,1,0:T(2,128)(2,1)} %copy.188, bf16[512,1,1,512]{3,2,1,0:T(2,128)(2,1)} %copy.187), kind=kLoop, calls=%fused_computation.56 | loop fusion | flops 2097152 | bytes 2097152 | tf_op jit(solution)/shard_map/stack | solution.py:129
  136.2 4.8 %all-to-all-start.3 = ((bf16[512,1,2,512]{3,2,1,0:T(2,128)(2,1)}), bf16[512,1,2,512]{3,2,1,0:T(2,128)(2,1)}, u32[]{:S(2)}, u32[]{:S(2)}) async-start(bf16[512,1,2,512]{3,2,1,0:T(2,128)(2,1)} %pad_maximum_fusion.2), calls=%async_computation.3 | async-start | bytes 2097152 | tf_op jit(solution)/shard_map/all_to_all | solution.py:151
  141.0 3.9 %fusion.27 = bf16[256,2,512]{2,0,1:T(8,128)(2,1)} fusion(bf16[2,512,1536]{1,2,0:T(8,128)(2,1)} %copy-done.4, bf16[2,1536,2,256]{3,1,2,0:T(8,128)(2,1)} %copy-done.1), kind=kOutput, calls=%fused_computation.51 | convolution fusion | flops 805830656 | bytes 4456448 | tf_op jit(solution)/shard_map/gqk,kd->qgd/dot_general | solution.py:70
  148.5 3.9 %fusion.28 = bf16[256,2,512]{2,0,1:T(8,128)(2,1)} fusion(bf16[2,512,1536]{1,2,0:T(8,128)(2,1)} %copy-done.5, bf16[2,1536,2,256]{3,1,2,0:T(8,128)(2,1)} %copy-done.1), kind=kOutput, calls=%fused_computation.52 | convolution fusion | flops 805830656 | bytes 4456448 | tf_op jit(solution)/shard_map/gqk,kd->qgd/dot_general | solution.py:70
  156.0 4.2 %pad_maximum_fusion.3 = bf16[512,1,2,512]{3,2,1,0:T(2,128)(2,1)} fusion(bf16[512,1,1,512]{3,2,1,0:T(2,128)(2,1)} %copy.201, bf16[512,1,1,512]{3,2,1,0:T(2,128)(2,1)} %copy.200), kind=kLoop, calls=%fused_computation.57 | loop fusion | flops 2097152 | bytes 2097152 | tf_op jit(solution)/shard_map/stack | solution.py:132
  160.2 4.8 %all-to-all-start.4 = ((bf16[512,1,2,512]{3,2,1,0:T(2,128)(2,1)}), bf16[512,1,2,512]{3,2,1,0:T(2,128)(2,1)}, u32[]{:S(2)}, u32[]{:S(2)}) async-start(bf16[512,1,2,512]{3,2,1,0:T(2,128)(2,1)} %pad_maximum_fusion.3), calls=%async_computation.4 | async-start | bytes 2097152 | tf_op jit(solution)/shard_map/all_to_all | solution.py:152
  167.3 29.7 %collective-permute-done.6 = f32[2,512,2,256]{3,1,0,2:T(8,128)} collective-permute-done((f32[2,512,2,256]{3,1,0,2:T(8,128)}, f32[2,512,2,256]{3,1,0,2:T(8,128)}, u32[]{:S(2)}, u32[]{:S(2)}) %collective-permute-start.6) | collective-permute-done | bytes 2097184 | tf_op jit(solution)/shard_map/ppermute | solution.py:30
  201.2 4.8 %all-to-all-start.6 = ((bf16[512,1,2,256]{3,2,1,0:T(2,128)(2,1)}), bf16[512,1,2,256]{3,2,1,0:T(2,128)(2,1)S(1)}, u32[]{:S(2)}, u32[]{:S(2)}) async-start(bf16[512,1,2,256]{3,2,1,0:T(2,128)(2,1)} %copy.209), calls=%async_computation.6 | async-start | bytes 1048576 | tf_op jit(solution)/shard_map/all_to_all | solution.py:154
  207.3 5.3 %all-to-all-done.6 = bf16[512,1,2,256]{3,2,1,0:T(2,128)(2,1)S(1)} async-done(((bf16[512,1,2,256]{3,2,1,0:T(2,128)(2,1)}), bf16[512,1,2,256]{3,2,1,0:T(2,128)(2,1)S(1)}, u32[]{:S(2)}, u32[]{:S(2)}) %all-to-all-start.6) | async-done | bytes 524320 | tf_op jit(solution)/shard_map/all_to_all | solution.py:154
  212.6 4.9 %all-to-all-start.5 = ((bf16[512,1,2,256]{3,2,1,0:T(2,128)(2,1)}), bf16[512,1,2,256]{3,2,1,0:T(2,128)(2,1)S(1)}, u32[]{:S(2)}, u32[]{:S(2)}) async-start(bf16[512,1,2,256]{3,2,1,0:T(2,128)(2,1)} %copy.207), calls=%async_computation.5 | async-start | bytes 1048576 | tf_op jit(solution)/shard_map/all_to_all | solution.py:153
  (108 shorter events, 74.7 us)
Async XLA Ops:
  0.6 7.4 %copy-start.10 = (bf16[128,4096]{1,0:T(8,128)(2,1)S(1)}, bf16[128,4096]{1,0:T(8,128)(2,1)}, u32[]{:S(2)}) copy-start(bf16[128,4096]{1,0:T(8,128)(2,1)} %param.8) | copy-start | bytes 3145732
  3.1 10.8 %copy-start.11 = (bf16[128,2048]{1,0:T(8,128)(2,1)S(1)}, bf16[128,2048]{1,0:T(8,128)(2,1)}, u32[]{:S(2)}) copy-start(bf16[128,2048]{1,0:T(8,128)(2,1)} %param.7) | copy-start | bytes 1572868
  3.1 17.6 %all-to-all-start = ((bf16[128,4,2,256]{3,0,2,1:T(8,128)(2,1)}), bf16[128,4,2,256]{3,0,2,1:T(8,128)(2,1)S(1)}, u32[]{:S(2)}, u32[]{:S(2)}) async-start(bf16[128,4,2,256]{3,0,2,1:T(8,128)(2,1)} %copy.171), calls=%async_computation | async-start | bytes 1048576 | tf_op jit(solution)/shard_map/all_to_all | solution.py:175
  8.7 18.3 %copy-start.14 = (s32[64]{0:T(128)S(1)}, s32[64]{0:T(128)}, u32[]{:S(2)}) copy-start(s32[64]{0:T(128)} %param.9) | copy-start | bytes 772
  9.8 41.5 %collective-permute-start.4 = (bf16[128,1,2,512]{0,3,2,1:T(8,128)(2,1)}, bf16[128,1,2,512]{0,3,2,1:T(8,128)(2,1)S(1)}, u32[]{:S(2)}, u32[]{:S(2)}) collective-permute-start(bf16[128,1,2,512]{0,3,2,1:T(8,128)(2,1)} %get-tuple-element.10), channel_id=1, source_target_pairs={{0,3},{1,2},{2,1},{3,0},{4,7},{5,6},{6,5},{7,4},{8,11},{9,10},{10,... | collective-permute-start | bytes 786440 | tf_op jit(solution)/shard_map/ppermute | solution.py:22
  11.2 39.0 %collective-permute-start.3 = (bf16[128,1,2,512]{0,3,2,1:T(8,128)(2,1)}, bf16[128,1,2,512]{0,3,2,1:T(8,128)(2,1)}, u32[]{:S(2)}, u32[]{:S(2)}) collective-permute-start(bf16[128,1,2,512]{0,3,2,1:T(8,128)(2,1)} %get-tuple-element.11), channel_id=1, source_target_pairs={{0,2},{1,3},{2,0},{3,1},{4,6},{5,7},{6,4},{7,5},{8,10},{9,11},{10,... | collective-permute-start | bytes 786440 | tf_op jit(solution)/shard_map/ppermute | solution.py:22
  11.8 37.4 %collective-permute-start.2 = (bf16[128,1,2,512]{0,3,2,1:T(8,128)(2,1)}, bf16[128,1,2,512]{0,3,2,1:T(8,128)(2,1)}, u32[]{:S(2)}, u32[]{:S(2)}) collective-permute-start(bf16[128,1,2,512]{0,3,2,1:T(8,128)(2,1)} %get-tuple-element.12), channel_id=1, source_target_pairs={{0,1},{1,0},{2,3},{3,2},{4,5},{5,4},{6,7},{7,6},{8,9},{9,8},{10,11... | collective-permute-start | bytes 786440 | tf_op jit(solution)/shard_map/ppermute | solution.py:22
  20.7 12.9 %all-to-all-start.1 = ((bf16[128,4,2,256]{3,0,2,1:T(8,128)(2,1)}), bf16[128,4,2,256]{3,0,2,1:T(8,128)(2,1)S(1)}, u32[]{:S(2)}, u32[]{:S(2)}) async-start(bf16[128,4,2,256]{3,0,2,1:T(8,128)(2,1)} %copy.174), calls=%async_computation.1 | async-start | bytes 1048576 | tf_op jit(solution)/shard_map/all_to_all | solution.py:176
  29.8 20.4 %copy-start.2 = (bf16[4,128,1,2,256]{4,1,0,3,2:T(8,128)(2,1)}, bf16[4,128,1,2,256]{4,1,0,3,2:T(8,128)(2,1)S(1)}, u32[]{:S(2)}) copy-start(bf16[4,128,1,2,256]{4,1,0,3,2:T(8,128)(2,1)S(1)} %copy.172) | copy-start | bytes 1572868
  33.6 18.8 %all-to-all-start.2 = ((bf16[128,4,2,512]{0,3,2,1:T(8,128)(2,1)}), bf16[128,4,2,512]{0,3,2,1:T(8,128)(2,1)S(1)}, u32[]{:S(2)}, u32[]{:S(2)}) async-start(bf16[128,4,2,512]{0,3,2,1:T(8,128)(2,1)} %bitcast.13), calls=%async_computation.2 | async-start | bytes 2097152 | tf_op jit(solution)/shard_map/all_to_all | solution.py:174
  40.5 25.1 %collective-permute-start.1 = (bf16[2,512,2,256]{3,1,2,0:T(8,128)(2,1)}, bf16[2,512,2,256]{3,1,2,0:T(8,128)(2,1)}, u32[]{:S(2)}, u32[]{:S(2)}) collective-permute-start(bf16[2,512,2,256]{3,1,2,0:T(8,128)(2,1)} %pad_maximum_fusion.1), channel_id=1, source_target_pairs={{0,4},{4,8},{8,12},{12,16},{16,20},{20,24},{24,28},{28,32},{32,36}... | collective-permute-start | bytes 3145736 | tf_op jit(solution)/shard_map/ppermute | solution.py:30
  42.4 28.6 %collective-permute-start = (bf16[2,512,2,256]{3,1,2,0:T(8,128)(2,1)}, bf16[2,512,2,256]{3,1,2,0:T(8,128)(2,1)}, u32[]{:S(2)}, u32[]{:S(2)}) collective-permute-start(bf16[2,512,2,256]{3,1,2,0:T(8,128)(2,1)} %pad_maximum_fusion.1), channel_id=1, source_target_pairs={{0,8},{4,12},{8,16},{12,20},{16,24},{20,28},{24,32},{28,36},{32,40... | collective-permute-start | bytes 3145736 | tf_op jit(solution)/shard_map/ppermute | solution.py:30
  73.2 31.1 %copy-start.1 = (bf16[2,1536,2,256]{3,1,2,0:T(8,128)(2,1)}, bf16[2,1536,2,256]{3,1,2,0:T(8,128)(2,1)S(1)}, u32[]{:S(2)}) copy-start(bf16[2,1536,2,256]{3,1,2,0:T(8,128)(2,1)S(1)} %maximum_maximum_fusion) | copy-start | bytes 9437188
  80.4 3.7 %copy-start.7 = (bf16[512,1,1,512]{0,3,2,1:T(8,128)(2,1)S(1)}, bf16[512,1,1,512]{0,3,2,1:T(8,128)(2,1)}, u32[]{:S(2)}) copy-start(bf16[512,1,1,512]{0,3,2,1:T(8,128)(2,1)} %get-tuple-element.8) | copy-start | bytes 1572868
  94.4 3.9 %copy-start.6 = (bf16[512,1,1,512]{0,3,2,1:T(8,128)(2,1)S(1)}, bf16[512,1,1,512]{0,3,2,1:T(8,128)(2,1)}, u32[]{:S(2)}) copy-start(bf16[512,1,1,512]{0,3,2,1:T(8,128)(2,1)} %get-tuple-element.9) | copy-start | bytes 1572868
  94.4 6.7 %slice-start = ((s8[6291456]{0:T(1024)(128)(4,1)}), s8[4194304]{0:T(1024)(128)(4,1)S(1)}, s32[]{:S(2)}) async-start(s8[6291456]{0:T(1024)(128)(4,1)} %bitcast.173), calls=%async_computation.7 | async-start | bytes 8388608
  100.1 4.2 %slice-start.2 = ((s8[6291456]{0:T(1024)(128)(4,1)}), s8[4194304]{0:T(1024)(128)(4,1)S(1)}, s32[]{:S(2)}) async-start(s8[6291456]{0:T(1024)(128)(4,1)} %bitcast.175), calls=%async_computation.9 | async-start | bytes 8388608
  101.2 3.1 %slice-start.3 = ((s8[6291456]{0:T(1024)(128)(4,1)}), s8[2097152]{0:T(1024)(128)(4,1)S(1)}, s32[]{:S(2)}) async-start(s8[6291456]{0:T(1024)(128)(4,1)} %bitcast.175), calls=%async_computation.10 | async-start | bytes 4194304
  112.1 55.2 %collective-permute-start.5 = (f32[2,512,2,256]{3,1,0,2:T(8,128)}, f32[2,512,2,256]{3,1,0,2:T(8,128)}, u32[]{:S(2)}, u32[]{:S(2)}) collective-permute-start(f32[2,512,2,256]{3,1,0,2:T(8,128)} %get-tuple-element.4), channel_id=1, source_target_pairs={{4,0},{8,4},{12,8},{16,12},{20,16},{24,20},{28,24},{32,28},{36,32}... | collective-permute-start | bytes 6291464 | tf_op jit(solution)/shard_map/ppermute | solution.py:30
  122.5 74.4 %collective-permute-start.6 = (f32[2,512,2,256]{3,1,0,2:T(8,128)}, f32[2,512,2,256]{3,1,0,2:T(8,128)}, u32[]{:S(2)}, u32[]{:S(2)}) collective-permute-start(f32[2,512,2,256]{3,1,0,2:T(8,128)} %get-tuple-element.5), channel_id=1, source_target_pairs={{8,0},{12,4},{16,8},{20,12},{24,16},{28,20},{32,24},{36,28},{40,32... | collective-permute-start | bytes 6291464 | tf_op jit(solution)/shard_map/ppermute | solution.py:30
  136.2 24.0 %all-to-all-start.3 = ((bf16[512,1,2,512]{3,2,1,0:T(2,128)(2,1)}), bf16[512,1,2,512]{3,2,1,0:T(2,128)(2,1)}, u32[]{:S(2)}, u32[]{:S(2)}) async-start(bf16[512,1,2,512]{3,2,1,0:T(2,128)(2,1)} %pad_maximum_fusion.2), calls=%async_computation.3 | async-start | bytes 2097152 | tf_op jit(solution)/shard_map/all_to_all | solution.py:151
  160.2 41.0 %all-to-all-start.4 = ((bf16[512,1,2,512]{3,2,1,0:T(2,128)(2,1)}), bf16[512,1,2,512]{3,2,1,0:T(2,128)(2,1)}, u32[]{:S(2)}, u32[]{:S(2)}) async-start(bf16[512,1,2,512]{3,2,1,0:T(2,128)(2,1)} %pad_maximum_fusion.3), calls=%async_computation.4 | async-start | bytes 2097152 | tf_op jit(solution)/shard_map/all_to_all | solution.py:152
  201.2 11.4 %all-to-all-start.6 = ((bf16[512,1,2,256]{3,2,1,0:T(2,128)(2,1)}), bf16[512,1,2,256]{3,2,1,0:T(2,128)(2,1)S(1)}, u32[]{:S(2)}, u32[]{:S(2)}) async-start(bf16[512,1,2,256]{3,2,1,0:T(2,128)(2,1)} %copy.209), calls=%async_computation.6 | async-start | bytes 1048576 | tf_op jit(solution)/shard_map/all_to_all | solution.py:154
  212.6 13.6 %all-to-all-start.5 = ((bf16[512,1,2,256]{3,2,1,0:T(2,128)(2,1)}), bf16[512,1,2,256]{3,2,1,0:T(2,128)(2,1)S(1)}, u32[]{:S(2)}, u32[]{:S(2)}) async-start(bf16[512,1,2,256]{3,2,1,0:T(2,128)(2,1)} %copy.207), calls=%async_computation.5 | async-start | bytes 1048576 | tf_op jit(solution)/shard_map/all_to_all | solution.py:153
  (9 other events, 16.8 us)
